TPU v7x, 32 devices: a whole 2x2x4 slice. The times are simulated.
32 devices in a mesh: dp: 8 (over z, y), ctx: 4 (over x, core).
Axes of the slice: x: 2, y: 2, z: 4, core: 2. Of those that a mesh axis runs over, the one named last changes fastest.
Arguments:
- tokens: bfloat16 [8, 512, 2048], P('dp', 'ctx'), may hold values from -6 to 6
- segment_ids: int32 [8, 512], P('dp', 'ctx'), may hold values from 0 to 2, as said below
- positions: int32 [8, 512], P('dp', 'ctx'), may hold values from 0 to 511, as said below
- attn_gain: bfloat16 [2048], P(('dp', 'ctx')), may hold values from 0.5 to 1.5
- w_query: bfloat16 [2048, 2048], P(('dp', 'ctx')), may hold values from -0.125 to 0.125
- w_key: bfloat16 [2048, 512], P(('dp', 'ctx')), may hold values from -0.125 to 0.125
- w_value: bfloat16 [2048, 512], P(('dp', 'ctx')), may hold values from -0.125 to 0.125
- w_output: bfloat16 [2048, 2048], P(('dp', 'ctx')), may hold values from -1 to 1
- ffn_gain: bfloat16 [2048], P(('dp', 'ctx')), may hold values from 0.5 to 1.5
- w_gate: bfloat16 [2048, 8192], P('dp', 'ctx'), may hold values from -0.125 to 0.125
- w_up: bfloat16 [2048, 8192], P('dp', 'ctx'), may hold values from -0.125 to 0.125
- w_down: bfloat16 [8192, 2048], P('ctx', 'dp'), may hold values from -0.125 to 0.125
- cotangent: bfloat16 [8, 512, 2048], P('dp', 'ctx'), may hold values from -6 to 6
Outputs:
- mixed: bfloat16 [8, 512, 2048], P('dp', 'ctx')
- grad_tokens: float32 [8, 512, 2048], P('dp', 'ctx')
- grad_attn_gain: float32 [2048], P(('dp', 'ctx'))
- grad_query: float32 [2048, 2048], P(('dp', 'ctx'))
- grad_key: float32 [2048, 512], P(('dp', 'ctx'))
- grad_value: float32 [2048, 512], P(('dp', 'ctx'))
- grad_output: float32 [2048, 2048], P(('dp', 'ctx'))
- grad_ffn_gain: float32 [2048], P(('dp', 'ctx'))
- grad_gate: float32 [2048, 8192], P('dp', 'ctx')
- grad_up: float32 [2048, 8192], P('dp', 'ctx')
- grad_down: float32 [8192, 2048], P('ctx', 'dp')
Inputs may be any that keep to these rules, and one draw needn't show every extreme that they name: `segment_ids`: along each packed sequence of 512 tokens the document number never falls and starts at 0; documents do not cross sequences. `positions`: 0 at a document's first token and rising by one along the document; the first packed sequence holds a single document.
All inputs are finite; a program needn't handle non-finite values.
Results may differ from a plain program's by a relative error of at most 0.018.
Values may be sent and summed in bfloat16 or wider, within the bound.
No kernel may reach another device: no remote copies, remote signals or barrier semaphores. Data moves between devices by JAX's collectives and lax.ppermute only.
A program may use at most 256 MiB of HBM per device.

v0:
```python
import jax
import jax.numpy as jnp
from jax import lax
from jax.sharding import PartitionSpec as P

QUERY_HEADS = 32
KEY_VALUE_HEADS = 8
HEAD_WIDTH = 64
EPS_NORM = 1e-05
ROPE_BASE = 500000.0
MASKED = -1e30


def rope_tables(where_pos, half_width):
    freqs = ROPE_BASE ** (-(jnp.arange(half_width, dtype=jnp.float32) / half_width))
    angles = where_pos.astype(jnp.float32)[..., None] * freqs
    return (jnp.cos(angles), jnp.sin(angles))


def apply_rotation(values, cosine_table, sine_table):
    half_width = values.shape[-1] // 2
    first = values[..., :half_width]
    second = values[..., half_width:]
    cosine_table = cosine_table[..., None, :]
    sine_table = sine_table[..., None, :]
    return jnp.concatenate(
        [first * cosine_table - second * sine_table, second * cosine_table + first * sine_table],
        axis=-1,
    )


def reverse_rotation(grads, cosine_table, sine_table):
    half_width = grads.shape[-1] // 2
    first = grads[..., :half_width]
    second = grads[..., half_width:]
    cosine_table = cosine_table[..., None, :]
    sine_table = sine_table[..., None, :]
    return jnp.concatenate(
        [first * cosine_table + second * sine_table, second * cosine_table - first * sine_table],
        axis=-1,
    )


def norm_back(upstream, normed, inverse, gain):
    scaled = upstream * gain
    return inverse * (scaled - normed * jnp.mean(scaled * normed, axis=-1, keepdims=True))


def tdot(left, right):
    return lax.dot_general(
        left, right, (((0,), (0,)), ((), ())), preferred_element_type=jnp.float32
    )


def body(
    tokens,
    segment_ids,
    positions,
    attn_gain,
    w_query,
    w_key,
    w_value,
    w_output,
    ffn_gain,
    w_gate,
    w_up,
    w_down,
    cotangent,
):
    local_sequence, context_rows, width = tokens.shape
    token_rows = local_sequence * context_rows
    count_ctx = lax.axis_size("ctx")
    sequence_length = context_rows * count_ctx
    group_rows = local_sequence * sequence_length
    query_groups = QUERY_HEADS // KEY_VALUE_HEADS
    factor = 1.0 / HEAD_WIDTH**0.5
    gain_one, gain_two, wquery, key_weight, value_weight, output_weight = (
        lax.all_gather(attn_gain, ("dp", "ctx"), axis=0, tiled=True),
        lax.all_gather(ffn_gain, ("dp", "ctx"), axis=0, tiled=True),
        lax.all_gather(w_query, ("dp", "ctx"), axis=0, tiled=True),
        lax.all_gather(w_key, ("dp", "ctx"), axis=0, tiled=True),
        lax.all_gather(w_value, ("dp", "ctx"), axis=0, tiled=True),
        lax.all_gather(w_output, ("dp", "ctx"), axis=0, tiled=True),
    )
    gain_onef = gain_one.astype(jnp.float32)
    gain_twof = gain_two.astype(jnp.float32)
    xfloat = tokens.reshape(token_rows, width).astype(jnp.float32)
    inv_one = lax.rsqrt(jnp.mean(xfloat * xfloat, axis=-1, keepdims=True) + EPS_NORM)
    normed_one = xfloat * inv_one
    hidden_first = (normed_one * gain_onef).astype(jnp.bfloat16)
    query_rows = jnp.dot(hidden_first, wquery, preferred_element_type=jnp.float32).reshape(
        local_sequence, context_rows, QUERY_HEADS, HEAD_WIDTH
    )
    unrotated_key = jnp.dot(hidden_first, key_weight, preferred_element_type=jnp.float32).reshape(
        local_sequence, context_rows, KEY_VALUE_HEADS, HEAD_WIDTH
    )
    value_own = (
        jnp.dot(hidden_first, value_weight, preferred_element_type=jnp.float32)
        .astype(jnp.bfloat16)
        .reshape(local_sequence, context_rows, KEY_VALUE_HEADS * HEAD_WIDTH)
    )
    cosine_table, sine_table = rope_tables(positions, HEAD_WIDTH // 2)
    rotated_query = (
        apply_rotation(query_rows, cosine_table, sine_table)
        .astype(jnp.bfloat16)
        .reshape(local_sequence, context_rows, KEY_VALUE_HEADS, query_groups, HEAD_WIDTH)
    )
    rkey_own = (
        apply_rotation(unrotated_key, cosine_table, sine_table)
        .astype(jnp.bfloat16)
        .reshape(local_sequence, context_rows, KEY_VALUE_HEADS * HEAD_WIDTH)
    )
    gathered_keys, gathered_values = (
        lax.all_gather(rkey_own, "ctx", axis=1, tiled=True),
        lax.all_gather(value_own, "ctx", axis=1, tiled=True),
    )
    segments_all = lax.all_gather(segment_ids, "ctx", axis=1, tiled=True)
    gathered_keys = gathered_keys.reshape(
        local_sequence, sequence_length, KEY_VALUE_HEADS, HEAD_WIDTH
    )
    gathered_values = gathered_values.reshape(
        local_sequence, sequence_length, KEY_VALUE_HEADS, HEAD_WIDTH
    )
    query_index = lax.axis_index("ctx") * context_rows + jnp.arange(context_rows, dtype=jnp.int32)
    key_index = jnp.arange(sequence_length, dtype=jnp.int32)
    allowed = (segment_ids[:, :, None] == segments_all[:, None, :]) & (
        key_index[None, None, :] <= query_index[None, :, None]
    )
    allowed = allowed[:, None, None]
    scores = (
        jnp.einsum(
            "schgd,slhd->shgcl", rotated_query, gathered_keys, preferred_element_type=jnp.float32
        )
        * factor
    )
    masked = jnp.where(allowed, scores, MASKED)
    expo = jnp.exp(masked)
    total = jnp.sum(expo, axis=-1, keepdims=True)
    lse = jnp.log(total)
    probs = (expo / total).astype(jnp.bfloat16)
    attended = jnp.einsum(
        "shgcl,slhd->schgd", probs, gathered_values, preferred_element_type=jnp.float32
    )
    attended = attended.astype(jnp.bfloat16).reshape(token_rows, QUERY_HEADS * HEAD_WIDTH)
    resid = xfloat + jnp.dot(attended, output_weight, preferred_element_type=jnp.float32)
    wgate, wup_proj, wdown = (
        lax.all_gather(w_gate, "dp", axis=0, tiled=True),
        lax.all_gather(w_up, "dp", axis=0, tiled=True),
        lax.all_gather(w_down, "dp", axis=1, tiled=True),
    )
    inv_two = lax.rsqrt(jnp.mean(resid * resid, axis=-1, keepdims=True) + EPS_NORM)
    normed_two = resid * inv_two
    h_two = (normed_two * gain_twof).astype(jnp.bfloat16)
    h_group, cot_group = (
        lax.all_gather(
            h_two.reshape(local_sequence, context_rows, width), "ctx", axis=1, tiled=True
        ),
        lax.all_gather(cotangent, "ctx", axis=1, tiled=True),
    )
    h_group = h_group.reshape(group_rows, width)
    cot_group = cot_group.reshape(group_rows, width)
    gate = jnp.dot(h_group, wgate, preferred_element_type=jnp.float32)
    up_proj = jnp.dot(h_group, wup_proj, preferred_element_type=jnp.float32)
    sigma = jax.nn.sigmoid(gate)
    hidden = (gate * sigma * up_proj).astype(jnp.bfloat16)
    partial_out = jnp.dot(hidden, wdown, preferred_element_type=jnp.float32).reshape(
        local_sequence, sequence_length, width
    )
    ffn_out = (
        lax.psum_scatter(partial_out.astype(jnp.bfloat16), "ctx", scatter_dimension=1, tiled=True)
        .astype(jnp.float32)
        .reshape(token_rows, width)
    )
    mixed = (resid + ffn_out).astype(jnp.bfloat16)
    cot_rows = cotangent.reshape(token_rows, width)
    d_hidden = jnp.dot(cot_group, wdown.T, preferred_element_type=jnp.float32)
    d_up = (d_hidden * gate * sigma).astype(jnp.bfloat16)
    d_gate = (d_hidden * up_proj * sigma * (1.0 + gate * (1.0 - sigma))).astype(jnp.bfloat16)
    ffn_sums = lax.psum_scatter(
        jnp.concatenate(
            [tdot(h_group, d_gate), tdot(h_group, d_up), tdot(cot_group, hidden)], axis=1
        ).astype(jnp.bfloat16),
        "dp",
        scatter_dimension=0,
        tiled=True,
    ).astype(jnp.float32)
    ff_width = w_gate.shape[1]
    grad_gate = ffn_sums[:, :ff_width]
    grad_up = ffn_sums[:, ff_width : 2 * ff_width]
    grad_down = ffn_sums[:, 2 * ff_width :].T
    d_h_part = jnp.dot(d_gate, wgate.T, preferred_element_type=jnp.float32) + jnp.dot(
        d_up, wup_proj.T, preferred_element_type=jnp.float32
    )
    d_h_two = (
        lax.psum_scatter(
            d_h_part.reshape(local_sequence, sequence_length, width).astype(jnp.bfloat16),
            "ctx",
            scatter_dimension=1,
            tiled=True,
        )
        .astype(jnp.float32)
        .reshape(token_rows, width)
    )
    gain_term_two = jnp.sum(d_h_two * normed_two, axis=0)
    d_resid = cot_rows.astype(jnp.float32) + norm_back(d_h_two, normed_two, inv_two, gain_twof)
    residual_gradient_second = d_resid.astype(jnp.bfloat16)
    out_term = tdot(attended, residual_gradient_second)
    attended_gradient = jnp.dot(
        residual_gradient_second, output_weight.T, preferred_element_type=jnp.float32
    ).astype(jnp.bfloat16)
    attended_gradient = attended_gradient.reshape(
        local_sequence, context_rows, KEY_VALUE_HEADS, query_groups, HEAD_WIDTH
    )
    probs_f = jnp.where(allowed, jnp.exp(masked - lse), 0.0)
    d_probs = jnp.einsum(
        "schgd,slhd->shgcl", attended_gradient, gathered_values, preferred_element_type=jnp.float32
    )
    delta = jnp.sum(probs_f * d_probs, axis=-1, keepdims=True)
    d_scores_b = (probs_f * (d_probs - delta) * factor).astype(jnp.bfloat16)
    value_gradient_local = jnp.einsum(
        "shgcl,schgd->slhd",
        probs_f.astype(jnp.bfloat16),
        attended_gradient,
        preferred_element_type=jnp.float32,
    )
    d_rquery = jnp.einsum(
        "shgcl,slhd->schgd", d_scores_b, gathered_keys, preferred_element_type=jnp.float32
    )
    rotated_key_gradient = jnp.einsum(
        "shgcl,schgd->slhd", d_scores_b, rotated_query, preferred_element_type=jnp.float32
    )
    key_gradient, value_gradient = (
        lax.psum_scatter(
            rotated_key_gradient.reshape(
                local_sequence, sequence_length, KEY_VALUE_HEADS * HEAD_WIDTH
            ).astype(jnp.bfloat16),
            "ctx",
            scatter_dimension=1,
            tiled=True,
        ).astype(jnp.float32),
        lax.psum_scatter(
            value_gradient_local.reshape(
                local_sequence, sequence_length, KEY_VALUE_HEADS * HEAD_WIDTH
            ).astype(jnp.bfloat16),
            "ctx",
            scatter_dimension=1,
            tiled=True,
        ).astype(jnp.float32),
    )
    dquery = (
        reverse_rotation(
            d_rquery.reshape(local_sequence, context_rows, QUERY_HEADS, HEAD_WIDTH),
            cosine_table,
            sine_table,
        )
        .astype(jnp.bfloat16)
        .reshape(token_rows, QUERY_HEADS * HEAD_WIDTH)
    )
    dkey = (
        reverse_rotation(
            key_gradient.reshape(local_sequence, context_rows, KEY_VALUE_HEADS, HEAD_WIDTH),
            cosine_table,
            sine_table,
        )
        .astype(jnp.bfloat16)
        .reshape(token_rows, KEY_VALUE_HEADS * HEAD_WIDTH)
    )
    value_gradient_full = value_gradient.astype(jnp.bfloat16).reshape(
        token_rows, KEY_VALUE_HEADS * HEAD_WIDTH
    )
    query_term = tdot(hidden_first, dquery)
    key_term = tdot(hidden_first, dkey)
    value_term = tdot(hidden_first, value_gradient_full)
    d_h_one = jnp.dot(dquery, wquery.T, preferred_element_type=jnp.float32)
    d_h_one = d_h_one + jnp.dot(dkey, key_weight.T, preferred_element_type=jnp.float32)
    d_h_one = d_h_one + jnp.dot(
        value_gradient_full, value_weight.T, preferred_element_type=jnp.float32
    )
    gain_term_one = jnp.sum(d_h_one * normed_one, axis=0)
    grad_tokens = d_resid + norm_back(d_h_one, normed_one, inv_one, gain_onef)
    summed = (
        lax.psum_scatter(gain_term_one, ("dp", "ctx"), scatter_dimension=0, tiled=True),
        lax.psum_scatter(gain_term_two, ("dp", "ctx"), scatter_dimension=0, tiled=True),
        lax.psum_scatter(query_term, ("dp", "ctx"), scatter_dimension=0, tiled=True),
        lax.psum_scatter(key_term, ("dp", "ctx"), scatter_dimension=0, tiled=True),
        lax.psum_scatter(value_term, ("dp", "ctx"), scatter_dimension=0, tiled=True),
        lax.psum_scatter(out_term, ("dp", "ctx"), scatter_dimension=0, tiled=True),
    )
    return (
        mixed.reshape(local_sequence, context_rows, width),
        grad_tokens.reshape(local_sequence, context_rows, width),
        summed[0],
        summed[2],
        summed[3],
        summed[4],
        summed[5],
        summed[1],
        grad_gate,
        grad_up,
        grad_down,
    )


def solution(mesh):
    return jax.shard_map(
        body,
        mesh=mesh,
        in_specs=(
            P("dp", "ctx", None),
            P("dp", "ctx"),
            P("dp", "ctx"),
            P(("dp", "ctx")),
            P(("dp", "ctx"), None),
            P(("dp", "ctx"), None),
            P(("dp", "ctx"), None),
            P(("dp", "ctx"), None),
            P(("dp", "ctx")),
            P("dp", "ctx"),
            P("dp", "ctx"),
            P("ctx", "dp"),
            P("dp", "ctx", None),
        ),
        out_specs=(
            P("dp", "ctx", None),
            P("dp", "ctx", None),
            P(("dp", "ctx")),
            P(("dp", "ctx"), None),
            P(("dp", "ctx"), None),
            P(("dp", "ctx"), None),
            P(("dp", "ctx"), None),
            P(("dp", "ctx")),
            P("dp", "ctx"),
            P("dp", "ctx"),
            P("ctx", "dp"),
        ),
        check_vma=False,
    )
```

profile of v0, /device:TPU:13, one launch (start us, length us, event | category | flops | bytes accessed | tf_op | source)
XLA Modules:
  0.0 1944.1 jit_solution(15713700508738842312)
XLA Ops:
  12.3 39.7 %all-reduce.5 = (bf16[2048]{0:T(1024)(128)(2,1)S(1)}, bf16[2048]{0:T(1024)(128)(2,1)S(1)}) all-reduce(bf16[2048]{0:T(1024)(128)(2,1)S(1)} %dynamic-update-slice, bf16[2048]{0:T(1024)(128)(2,1)S(1)} %dynamic-update-slice.1), channel_id=1, replica_groups=mesh['dp'=8,'ctx'=4] {'dp','ctx'}, use_global_device_ids=true, to_apply=%add | all-reduce | flops 4096 | bytes 16384
  52.1 7.6 all_gather.47
  70.1 7.3 all-gather
  78.4 47.4 %all-gather.14.cloned.1.call-done = bf16[2048,512]{1,0:T(8,128)(2,1)} async-done(((bf16[64,512]{1,0:T(8,128)(2,1)}), bf16[2048,512]{1,0:T(8,128)(2,1)}) %all-gather.14.cloned.1.call-update) | async-done | bytes 2097168 | tf_op jit(solution)/shard_map/all_gather | solution.py:81
  129.6 7.3 all_gather.50
  136.9 68.7 %all-gather.16.cloned.1.call-done = bf16[2048,2048]{1,0:T(8,128)(2,1)} async-done(((bf16[64,2048]{1,0:T(8,128)(2,1)}), bf16[2048,2048]{1,0:T(8,128)(2,1)}) %all-gather.16.cloned.1.call-update) | async-done | bytes 8388624 | tf_op jit(solution)/shard_map/all_gather | solution.py:80
  205.6 12.3 copy.48
  231.4 52.5 %all-gather.18.cloned.1.call-done = bf16[2048,2048]{1,0:T(8,128)(2,1)} async-done(((bf16[64,2048]{1,0:T(8,128)(2,1)}), bf16[2048,2048]{1,0:T(8,128)(2,1)}) %all-gather.18.cloned.1.call-update) | async-done | bytes 8388624 | tf_op jit(solution)/shard_map/all_gather | solution.py:83
  292.3 113.1 %all-gather.20.cloned.1.call-done = bf16[2048,2048]{1,0:T(8,128)(2,1)} async-done(((bf16[256,2048]{1,0:T(8,128)(2,1)}), bf16[2048,2048]{1,0:T(8,128)(2,1)}) %all-gather.20.cloned.1.call-update) | async-done | bytes 8388624 | tf_op jit(solution)/shard_map/all_gather | solution.py:147
  405.3 26.4 %all-gather.28.cloned.1.call-done = bf16[512,2048]{1,0:T(8,128)(2,1)} async-done(((bf16[128,2048]{1,0:T(8,128)(2,1)}), bf16[512,2048]{1,0:T(8,128)(2,1)}) %all-gather.28.cloned.1.call-update) | async-done | bytes 2097168 | tf_op jit(solution)/shard_map/all_gather | solution.py:155
  431.8 10.5 fusion.80
  442.3 112.5 %all-gather.22.cloned.1.call-done = bf16[2048,2048]{1,0:T(8,128)(2,1)} async-done(((bf16[256,2048]{1,0:T(8,128)(2,1)}), bf16[2048,2048]{1,0:T(8,128)(2,1)}) %all-gather.22.cloned.1.call-update) | async-done | bytes 8388624 | tf_op jit(solution)/shard_map/all_gather | solution.py:148
  554.7 10.5 fusion.81
  565.2 15.5 all-gather.26.cloned.1.call-done
  580.8 123.3 %all-gather.24.cloned.1.call-done = bf16[2048,2048]{1,0:T(8,128)(2,1)} async-done(((bf16[2048,256]{1,0:T(8,128)(2,1)}), bf16[2048,2048]{1,0:T(8,128)(2,1)}) %all-gather.24.cloned.1.call-update) | async-done | bytes 8388624 | tf_op jit(solution)/shard_map/all_gather | solution.py:149
  704.1 12.1 multiply_convert_fusion
  716.2 8.0 fusion.82
  724.2 7.4 fusion.11
  731.7 9.9 fusion.10
  741.6 9.6 reduce-scatter.28.cloned.1.call-start
  751.2 10.1 convolution_convert_fusion
  770.2 27.9 %reduce-scatter.14.cloned.1.call-done = bf16[1,128,2048]{2,1,0:T(8,128)(2,1)} async-done(((bf16[1,512,2048]{2,1,0:T(8,128)(2,1)}), bf16[1,128,2048]{2,1,0:T(8,128)(2,1)}) %reduce-scatter.14.cloned.1.call-update) | async-done | bytes 524304 | tf_op jit(solution)/shard_map/reduce_scatter | solution.py:170
  824.9 10.0 convolution_convert_fusion.1
  844.5 19.0 pad_maximum_fusion
  878.8 9.1 fusion.52
  888.0 8.1 fusion.61
  905.2 41.9 %all-reduce.4 = (f32[2048]{0:T(1024)S(1)}, f32[2048]{0:T(1024)S(1)}) all-reduce(f32[2048]{0:T(1024)S(1)} %get-tuple-element.46, f32[2048]{0:T(1024)S(1)} %get-tuple-element.44), channel_id=8, replica_groups=mesh['dp'=8,'ctx'=4] {'dp','ctx'}, use_global_device_ids=true, to_apply=%region_11.12.clone | all-reduce | flops 4096 | bytes 32768
  949.6 328.6 %reduce-scatter.26.cloned.1.call-done = bf16[256,6144]{0,1:T(8,128)(2,1)} async-done(((bf16[2048,6144]{0,1:T(8,128)(2,1)}), bf16[256,6144]{0,1:T(8,128)(2,1)}) %reduce-scatter.26.cloned.1.call-update) | async-done | bytes 3145744 | tf_op jit(solution)/shard_map/reduce_scatter | solution.py:179
  1289.9 101.7 %reduce-scatter.20.cloned.1.call-done = f32[64,512]{1,0:T(8,128)} async-done(((f32[2048,512]{1,0:T(8,128)}), f32[64,512]{1,0:T(8,128)}) %reduce-scatter.20.cloned.1.call-update) | async-done | bytes 131088 | tf_op jit(solution)/shard_map/reduce_scatter | solution.py:285
  1391.5 141.5 %reduce-scatter.22.cloned.1.call-done = f32[64,512]{1,0:T(8,128)} async-done(((f32[2048,512]{1,0:T(8,128)}), f32[64,512]{1,0:T(8,128)}) %reduce-scatter.22.cloned.1.call-update) | async-done | bytes 131088 | tf_op jit(solution)/shard_map/reduce_scatter | solution.py:286
  1533.1 216.4 %reduce-scatter.18.cloned.1.call-done = f32[64,2048]{1,0:T(8,128)} async-done(((f32[2048,2048]{1,0:T(8,128)}), f32[64,2048]{1,0:T(8,128)}) %reduce-scatter.18.cloned.1.call-update) | async-done | bytes 524304 | tf_op jit(solution)/shard_map/reduce_scatter | solution.py:284
  1749.5 187.4 %reduce-scatter.24.cloned.1.call-done = f32[64,2048]{1,0:T(8,128)} async-done(((f32[2048,2048]{1,0:T(8,128)}), f32[64,2048]{1,0:T(8,128)}) %reduce-scatter.24.cloned.1.call-update) | async-done | bytes 524304 | tf_op jit(solution)/shard_map/reduce_scatter | solution.py:287
  (145 shorter events, 125.7 us)
Async XLA Ops:
  7.2 60.6 %all-gather.12.cloned.1.call-start = ((), (), s32[]{:S(2)}) async-start(), calls=%async_computation.9 | async-start | bytes 2162688 | tf_op jit(solution)/shard_map/all_gather | solution.py:82
  7.9 117.8 %all-gather.14.cloned.1.call-start = ((), (), s32[]{:S(2)}) async-start(), calls=%async_computation.10 | async-start | bytes 2162688 | tf_op jit(solution)/shard_map/all_gather | solution.py:81
  8.7 196.9 %all-gather.16.cloned.1.call-start = ((), (), s32[]{:S(2)}) async-start(), calls=%async_computation.11 | async-start | bytes 8650752 | tf_op jit(solution)/shard_map/all_gather | solution.py:80
  9.4 274.6 %all-gather.18.cloned.1.call-start = ((), (), s32[]{:S(2)}) async-start(), calls=%async_computation.12 | async-start | bytes 8650752 | tf_op jit(solution)/shard_map/all_gather | solution.py:83
  10.0 395.4 %all-gather.20.cloned.1.call-start = ((), (), s32[]{:S(2)}) async-start(), calls=%async_computation.13 | async-start | bytes 9437184 | tf_op jit(solution)/shard_map/all_gather | solution.py:147
  10.6 421.2 %all-gather.28.cloned.1.call-start = ((), (), s32[]{:S(2)}) async-start(), calls=%async_computation.24 | async-start | bytes 2621440 | tf_op jit(solution)/shard_map/all_gather | solution.py:155
  62.5 66.1 %copy-start.1 = (bf16[1,128,2048]{2,1,0:T(8,128)(2,1)S(1)}, bf16[1,128,2048]{2,1,0:T(8,128)(2,1)}, u32[]{:S(2)}) copy-start(bf16[1,128,2048]{2,1,0:T(8,128)(2,1)} %param.13) | copy-start | bytes 1572868
  136.9 87.1 %copy-start.4 = (bf16[1,512,512]{1,2,0:T(8,128)(2,1)}, bf16[1,512,512]{1,2,0:T(8,128)(2,1)S(1)}, u32[]{:S(2)}) copy-start(bf16[1,512,512]{1,2,0:T(8,128)(2,1)S(1)} %all_gather.50) | copy-start | bytes 1572868
  223.9 5.4 copy-start.9
  226.0 5.4 copy-start.12
  289.7 265.0 %all-gather.22.cloned.1.call-start = ((), (), s32[]{:S(2)}) async-start(), calls=%async_computation.14 | async-start | bytes 9437184 | tf_op jit(solution)/shard_map/all_gather | solution.py:148
  290.5 290.3 %all-gather.26.cloned.1.call-start = ((), (), s32[]{:S(2)}) async-start(), calls=%async_computation.17 | async-start | bytes 2621440 | tf_op jit(solution)/shard_map/all_gather | solution.py:158
  291.2 412.9 %all-gather.24.cloned.1.call-start = ((), (), s32[]{:S(2)}) async-start(), calls=%async_computation.15 | async-start | bytes 9437184 | tf_op jit(solution)/shard_map/all_gather | solution.py:149
  292.0 476.2 %reduce-scatter.16.cloned.1.call-start = ((), (), s32[]{:S(2)}) async-start(), calls=%async_computation.18 | async-start | bytes 2621440 | tf_op jit(solution)/shard_map/reduce_scatter | solution.py:195
  716.2 8.0 copy-start.16
  716.2 8.0 copy-start.14
  731.6 66.4 %reduce-scatter.14.cloned.1.call-start = ((), (), s32[]{:S(2)}) async-start(), calls=%async_computation.16 | async-start | bytes 2621440 | tf_op jit(solution)/shard_map/reduce_scatter | solution.py:170
  731.7 19.5 %copy-start.13 = (f32[8,4,128]{2,1,0:T(4,128)S(1)}, f32[8,4,128]{2,1,0:T(4,128)}, u32[]{:S(2)}) copy-start(f32[8,4,128]{2,1,0:T(4,128)} %copy-done.12) | copy-start | bytes 49156
  741.6 122.1 %reduce-scatter.28.cloned.1.call-start = ((), (), s32[]{:S(2)}) async-start(), calls=%async_computation.25 | async-start | bytes 655360
  751.2 10.2 copy-start.15
  751.2 10.2 copy-start.17
  800.6 7.3 copy-start.10
  807.9 5.2 slice-start
  807.9 6.1 slice-start.1
  824.6 10.3 copy-start.11
  824.7 46.5 %reduce-scatter.30.cloned.1.call-start = ((), (), s32[]{:S(2)}) async-start(), calls=%async_computation.26 | async-start | bytes 655360
  844.5 433.7 %reduce-scatter.26.cloned.1.call-start = ((), (), s32[]{:S(2)}) async-start(), calls=%async_computation.23 | async-start | bytes 28311552 | tf_op jit(solution)/shard_map/reduce_scatter | solution.py:179
  863.6 528.0 %reduce-scatter.20.cloned.1.call-start = ((), (), s32[]{:S(2)}) async-start(), calls=%async_computation.20 | async-start | bytes 4325376 | tf_op jit(solution)/shard_map/reduce_scatter | solution.py:285
  867.8 665.3 %reduce-scatter.22.cloned.1.call-start = ((), (), s32[]{:S(2)}) async-start(), calls=%async_computation.21 | async-start | bytes 4325376 | tf_op jit(solution)/shard_map/reduce_scatter | solution.py:286
  875.3 874.2 %reduce-scatter.18.cloned.1.call-start = ((), (), s32[]{:S(2)}) async-start(), calls=%async_computation.19 | async-start | bytes 17301504 | tf_op jit(solution)/shard_map/reduce_scatter | solution.py:284
  887.9 1048.9 %reduce-scatter.24.cloned.1.call-start = ((), (), s32[]{:S(2)}) async-start(), calls=%async_computation.22 | async-start | bytes 17301504 | tf_op jit(solution)/shard_map/reduce_scatter | solution.py:287
  896.1 6.5 copy-start.3
  (6 other events, 17.3 us)
Sparse Core Ops, SparseCore 0:
  10.8 56.9 all-gather.11
  70.7 55.0 all-gather.13
  128.6 76.8 all-gather.15
  208.3 75.6 all-gather.17
  285.9 119.3 all-gather.19
  407.3 24.4 all-gather.27
  433.9 120.7 all-gather.21
  556.3 24.4 all-gather.25
  582.8 121.2 all-gather.23
  731.7 32.4 reduce-scatter.15
  766.8 31.1 reduce-scatter.13
  824.8 21.6 reduce-scatter.27
  849.5 21.6 reduce-scatter.29
  874.9 403.1 reduce-scatter.25
  1280.9 110.6 reduce-scatter.19
  1394.3 138.7 reduce-scatter.21
  1535.8 213.6 reduce-scatter.17
  1752.2 184.5 reduce-scatter.23
where the time goes:
time: 1950 us; the launch traced here: 1940 us
  waiting for transfers between devices  1580 us (81%)
  matrix products  157 us (8%)
  blocking collectives  104 us (5%)
  local copies, waits for them, and re-layouts  45.6 us (2%)
  other arithmetic  34.6 us (2%)
    reduce_scatter x1, waiting for transfers between devices, body(): lax.psum_scatter(jnp.concatenate([tdot(h_group, d_gate), tdot(h_group, d_...  329 us
    reduce_scatter x1, waiting for transfers between devices, body(): lax.psum_scatter(query_term, ('dp', 'ctx'), scatter_dimension=0, tiled=True)  216 us
    reduce_scatter x1, waiting for transfers between devices, body(): lax.psum_scatter(out_term, ('dp', 'ctx'), scatter_dimension=0, tiled=True)  187 us
    reduce_scatter x1, waiting for transfers between devices, body(): lax.psum_scatter(value_term, ('dp', 'ctx'), scatter_dimension=0, tiled=True)  142 us
    all_gather x1, waiting for transfers between devices, body(): lax.all_gather(w_down, 'dp', axis=1, tiled=True)  123 us
    all_gather x1, waiting for transfers between devices, body(): lax.all_gather(w_gate, 'dp', axis=0, tiled=True)  113 us
    all_gather x1, waiting for transfers between devices, body(): lax.all_gather(w_up, 'dp', axis=0, tiled=True)  112 us
    reduce_scatter x1, waiting for transfers between devices, body(): lax.psum_scatter(key_term, ('dp', 'ctx'), scatter_dimension=0, tiled=True)  102 us
  transfers between devices with their start and end apart: 18, of which 16 were waited for; matrix products, arithmetic and copies ran while one was open for 9% of the time, Pallas kernels for 0%

commit v1 on v0

--- a/solution.py
+++ b/solution.py
@@ -9,6 +9,23 @@
 EPS_NORM = 1e-05
 ROPE_BASE = 500000.0
 MASKED = -1e30
+
+
+def in_order(blocks, dim):
+    blocks = jnp.moveaxis(blocks, 0, dim)
+    lengths = blocks.shape
+    return blocks.reshape(*lengths[:dim], lengths[dim] * lengths[dim + 1], *lengths[dim + 2 :])
+
+
+def collect(x, axis, dim):
+    peers = lax.axis_size(axis)
+    upward = [(i, (i + 1) % peers) for i in range(peers)]
+    blocks = [x]
+    while len(blocks) < peers:
+        blocks.append(lax.ppermute(blocks[-1], axis, upward))
+    index = lax.axis_index(axis)
+    blocks = jnp.stack(blocks)[(index - jnp.arange(peers)) % peers]
+    return in_order(blocks, dim)
 
 
 def rope_tables(where_pos, half_width):
@@ -145,7 +162,7 @@
     resid = xfloat + jnp.dot(attended, output_weight, preferred_element_type=jnp.float32)
     wgate, wup_proj, wdown = (
         lax.all_gather(w_gate, "dp", axis=0, tiled=True),
-        lax.all_gather(w_up, "dp", axis=0, tiled=True),
+        collect(w_up, "dp", 0),
         lax.all_gather(w_down, "dp", axis=1, tiled=True),
     )
     inv_two = lax.rsqrt(jnp.mean(resid * resid, axis=-1, keepdims=True) + EPS_NORM)

time: 1950 us -> 1880 us (0.964)
  waiting for transfers between devices: 1580 us -> 1470 us
  local copies, waits for them, and re-layouts: 45.6 us -> 66.8 us
    all_gather x1 -> x0, waiting for transfers between devices: 112 us -> none  [body(): lax.all_gather(w_up, 'dp', axis=0, tiled=True)]
    ppermute x0 -> x7, waiting for transfers between devices: none -> 82.4 us  [collect(): blocks.append(lax.ppermute(blocks[-1], axis, upward))]
    all_gather x1, waiting for transfers between devices: 47.4 us -> 0.01 us  [body(): lax.all_gather(w_key, ('dp', 'ctx'), axis=0, tiled=True)]
    reduce_scatter x1, waiting for transfers between devices: 142 us -> 101 us  [body(): lax.psum_scatter(value_term, ('dp', 'ctx'), scatter_dimension=0, tiled=True)]
    reduce_scatter x1, waiting for transfers between devices: 102 us -> 141 us  [body(): lax.psum_scatter(key_term, ('dp', 'ctx'), scatter_dimension=0, tiled=True)]
    reduce_scatter x1, waiting for transfers between devices: 187 us -> 217 us  [body(): lax.psum_scatter(out_term, ('dp', 'ctx'), scatter_dimension=0, tiled=True)]
    reduce_scatter x1, waiting for transfers between devices: 216 us -> 187 us  [body(): lax.psum_scatter(query_term, ('dp', 'ctx'), scatter_dimension=0, tiled=True)]
  transfers between devices with their start and end apart: 18 -> 24, of which waited for: 16 -> 17; matrix products, arithmetic and copies ran while one was open for 9% -> 10% of each run, Pallas kernels for 0% -> 0%
where the time goes in v1:
time: 1880 us
  waiting for transfers between devices  1470 us (78%)
  matrix products  149 us (8%)
  blocking collectives  122 us (6%)
  local copies, waits for them, and re-layouts  66.8 us (4%)
  other arithmetic  37.5 us (2%)
    reduce_scatter x1, waiting for transfers between devices, body(): lax.psum_scatter(jnp.concatenate([tdot(h_group, d_gate), tdot(h_group, d_...  329 us
    reduce_scatter x1, waiting for transfers between devices, body(): lax.psum_scatter(out_term, ('dp', 'ctx'), scatter_dimension=0, tiled=True)  217 us
    reduce_scatter x1, waiting for transfers between devices, body(): lax.psum_scatter(query_term, ('dp', 'ctx'), scatter_dimension=0, tiled=True)  187 us
    reduce_scatter x1, waiting for transfers between devices, body(): lax.psum_scatter(key_term, ('dp', 'ctx'), scatter_dimension=0, tiled=True)  141 us
    all_gather x1, waiting for transfers between devices, body(): lax.all_gather(w_gate, 'dp', axis=0, tiled=True)  114 us
    all_gather x1, waiting for transfers between devices, body(): lax.all_gather(w_down, 'dp', axis=1, tiled=True)  105 us
    reduce_scatter x1, waiting for transfers between devices, body(): lax.psum_scatter(value_term, ('dp', 'ctx'), scatter_dimension=0, tiled=True)  101 us
    unnamed x2, blocking collectives  99.2 us
  transfers between devices with their start and end apart: 24, of which 17 were waited for; matrix products, arithmetic and copies ran while one was open for 10% of the time, Pallas kernels for 0%

profile of v1, /device:TPU:13, one launch (start us, length us, event | category | flops | bytes accessed | tf_op | source)
XLA Modules:
  0.0 1877.1 jit_solution(15910090893129224082)
XLA Ops:
  13.2 23.5 %collective-permute-done = bf16[256,2048]{1,0:T(8,128)(2,1)S(1)} collective-permute-done((bf16[256,2048]{1,0:T(8,128)(2,1)}, bf16[256,2048]{1,0:T(8,128)(2,1)S(1)}, u32[]{:S(2)}, u32[]{:S(2)}) %collective-permute-start) | collective-permute-done | bytes 1048608 | tf_op jit(solution)/shard_map/ppermute | solution.py:25
  48.5 15.0 collective-permute-done.1
  70.0 22.9 %collective-permute-done.2 = bf16[256,2048]{1,0:T(8,128)(2,1)S(1)} collective-permute-done((bf16[256,2048]{1,0:T(8,128)(2,1)}, bf16[256,2048]{1,0:T(8,128)(2,1)S(1)}, u32[]{:S(2)}, u32[]{:S(2)}) %collective-permute-start.2) | collective-permute-done | bytes 1048608 | tf_op jit(solution)/shard_map/ppermute | solution.py:25
  97.7 57.3 %all-reduce.5 = (bf16[2048]{0:T(1024)(128)(2,1)S(1)}, bf16[2048]{0:T(1024)(128)(2,1)S(1)}) all-reduce(bf16[2048]{0:T(1024)(128)(2,1)S(1)} %dynamic-update-slice, bf16[2048]{0:T(1024)(128)(2,1)S(1)} %dynamic-update-slice.1), channel_id=1, replica_groups=mesh['dp'=8,'ctx'=4] {'dp','ctx'}, use_global_device_ids=true, to_apply=%add | all-reduce | flops 4096 | bytes 16384
  163.0 8.6 all-gather
  191.6 65.1 %all-gather.15.cloned.1.call-done = bf16[2048,2048]{1,0:T(8,128)(2,1)} async-done(((bf16[64,2048]{1,0:T(8,128)(2,1)}), bf16[2048,2048]{1,0:T(8,128)(2,1)}) %all-gather.15.cloned.1.call-update) | async-done | bytes 8388624 | tf_op jit(solution)/shard_map/all_gather | solution.py:97
  256.7 12.4 copy.48
  282.8 55.2 %all-gather.17.cloned.1.call-done = bf16[2048,2048]{1,0:T(8,128)(2,1)} async-done(((bf16[64,2048]{1,0:T(8,128)(2,1)}), bf16[2048,2048]{1,0:T(8,128)(2,1)}) %all-gather.17.cloned.1.call-update) | async-done | bytes 8388624 | tf_op jit(solution)/shard_map/all_gather | solution.py:100
  354.1 17.0 collective-permute-done.6
  372.1 8.3 gather_fusion
  380.5 104.5 %all-gather.21.cloned.1.call-done = bf16[2048,2048]{1,0:T(8,128)(2,1)} async-done(((bf16[2048,256]{1,0:T(8,128)(2,1)}), bf16[2048,2048]{1,0:T(8,128)(2,1)}) %all-gather.21.cloned.1.call-update) | async-done | bytes 8388624 | tf_op jit(solution)/shard_map/all_gather | solution.py:166
  485.0 10.6 fusion.13
  495.6 114.3 %all-gather.19.cloned.1.call-done = bf16[2048,2048]{1,0:T(8,128)(2,1)} async-done(((bf16[256,2048]{1,0:T(8,128)(2,1)}), bf16[2048,2048]{1,0:T(8,128)(2,1)}) %all-gather.19.cloned.1.call-update) | async-done | bytes 8388624 | tf_op jit(solution)/shard_map/all_gather | solution.py:164
  609.8 26.6 %all-gather.25.cloned.1.call-done = bf16[512,2048]{1,0:T(8,128)(2,1)} async-done(((bf16[128,2048]{1,0:T(8,128)(2,1)}), bf16[512,2048]{1,0:T(8,128)(2,1)}) %all-gather.25.cloned.1.call-update) | async-done | bytes 2097168 | tf_op jit(solution)/shard_map/all_gather | solution.py:172
  636.4 7.7 fusion.82
  644.1 11.3 multiply_convert_fusion
  655.4 7.9 fusion.83
  663.4 7.8 fusion.11
  671.3 9.9 fusion.10
  681.2 10.2 convolution_convert_fusion
  706.8 28.7 %reduce-scatter.14.cloned.1.call-done = bf16[1,128,2048]{2,1,0:T(8,128)(2,1)} async-done(((bf16[1,512,2048]{2,1,0:T(8,128)(2,1)}), bf16[1,128,2048]{2,1,0:T(8,128)(2,1)}) %reduce-scatter.14.cloned.1.call-update) | async-done | bytes 524304 | tf_op jit(solution)/shard_map/reduce_scatter | solution.py:187
  758.1 7.6 fusion.4
  771.1 18.0 pad_maximum_fusion
  793.4 11.1 reduce-scatter.28.cloned.1.call-done
  808.7 9.0 fusion.61
  822.0 8.2 fusion.52
  838.6 41.9 %all-reduce.4 = (f32[2048]{0:T(1024)S(1)}, f32[2048]{0:T(1024)S(1)}) all-reduce(f32[2048]{0:T(1024)S(1)} %get-tuple-element.46, f32[2048]{0:T(1024)S(1)} %get-tuple-element.44), channel_id=8, replica_groups=mesh['dp'=8,'ctx'=4] {'dp','ctx'}, use_global_device_ids=true, to_apply=%region_11.12.clone | all-reduce | flops 4096 | bytes 32768
  883.0 328.6 %reduce-scatter.26.cloned.1.call-done = bf16[256,6144]{0,1:T(8,128)(2,1)} async-done(((bf16[2048,6144]{0,1:T(8,128)(2,1)}), bf16[256,6144]{0,1:T(8,128)(2,1)}) %reduce-scatter.26.cloned.1.call-update) | async-done | bytes 3145744 | tf_op jit(solution)/shard_map/reduce_scatter | solution.py:196
  1223.3 101.4 %reduce-scatter.22.cloned.1.call-done = f32[64,512]{1,0:T(8,128)} async-done(((f32[2048,512]{1,0:T(8,128)}), f32[64,512]{1,0:T(8,128)}) %reduce-scatter.22.cloned.1.call-update) | async-done | bytes 131088 | tf_op jit(solution)/shard_map/reduce_scatter | solution.py:303
  1324.8 141.4 %reduce-scatter.20.cloned.1.call-done = f32[64,512]{1,0:T(8,128)} async-done(((f32[2048,512]{1,0:T(8,128)}), f32[64,512]{1,0:T(8,128)}) %reduce-scatter.20.cloned.1.call-update) | async-done | bytes 131088 | tf_op jit(solution)/shard_map/reduce_scatter | solution.py:302
  1466.2 216.7 %reduce-scatter.24.cloned.1.call-done = f32[64,2048]{1,0:T(8,128)} async-done(((f32[2048,2048]{1,0:T(8,128)}), f32[64,2048]{1,0:T(8,128)}) %reduce-scatter.24.cloned.1.call-update) | async-done | bytes 524304 | tf_op jit(solution)/shard_map/reduce_scatter | solution.py:304
  1682.9 187.4 %reduce-scatter.18.cloned.1.call-done = f32[64,2048]{1,0:T(8,128)} async-done(((f32[2048,2048]{1,0:T(8,128)}), f32[64,2048]{1,0:T(8,128)}) %reduce-scatter.18.cloned.1.call-update) | async-done | bytes 524304 | tf_op jit(solution)/shard_map/reduce_scatter | solution.py:301
  (198 shorter events, 166.1 us)
Async XLA Ops:
  7.2 153.7 %copy-start.1 = (bf16[1,128,2048]{2,1,0:T(8,128)(2,1)S(1)}, bf16[1,128,2048]{2,1,0:T(8,128)(2,1)}, u32[]{:S(2)}) copy-start(bf16[1,128,2048]{2,1,0:T(8,128)(2,1)} %param.13) | copy-start | bytes 1572868
  7.2 153.7 %all-gather.11.cloned.1.call-start = ((), (), s32[]{:S(2)}) async-start(), calls=%async_computation.9 | async-start | bytes 2162688 | tf_op jit(solution)/shard_map/all_gather | solution.py:99
  7.9 164.7 %all-gather.13.cloned.1.call-start = ((), (), s32[]{:S(2)}) async-start(), calls=%async_computation.10 | async-start | bytes 2162688 | tf_op jit(solution)/shard_map/all_gather | solution.py:98
  8.7 248.1 %all-gather.15.cloned.1.call-start = ((), (), s32[]{:S(2)}) async-start(), calls=%async_computation.11 | async-start | bytes 8650752 | tf_op jit(solution)/shard_map/all_gather | solution.py:97
  9.4 328.6 %all-gather.17.cloned.1.call-start = ((), (), s32[]{:S(2)}) async-start(), calls=%async_computation.12 | async-start | bytes 8650752 | tf_op jit(solution)/shard_map/all_gather | solution.py:100
  10.0 370.5 %all-gather.23.cloned.1.call-start = ((), (), s32[]{:S(2)}) async-start(), calls=%async_computation.16 | async-start | bytes 2621440 | tf_op jit(solution)/shard_map/all_gather | solution.py:175
  10.6 474.4 %all-gather.21.cloned.1.call-start = ((), (), s32[]{:S(2)}) async-start(), calls=%async_computation.14 | async-start | bytes 9437184 | tf_op jit(solution)/shard_map/all_gather | solution.py:166
  11.1 598.7 %all-gather.19.cloned.1.call-start = ((), (), s32[]{:S(2)}) async-start(), calls=%async_computation.13 | async-start | bytes 9437184 | tf_op jit(solution)/shard_map/all_gather | solution.py:164
  11.9 624.5 %all-gather.25.cloned.1.call-start = ((), (), s32[]{:S(2)}) async-start(), calls=%async_computation.23 | async-start | bytes 2621440 | tf_op jit(solution)/shard_map/all_gather | solution.py:172
  11.9 24.8 %collective-permute-start = (bf16[256,2048]{1,0:T(8,128)(2,1)}, bf16[256,2048]{1,0:T(8,128)(2,1)S(1)}, u32[]{:S(2)}, u32[]{:S(2)}) collective-permute-start(bf16[256,2048]{1,0:T(8,128)(2,1)} %param.23), channel_id=1, source_target_pairs={{0,4},{4,8},{8,12},{12,16},{16,20},{20,24},{24,28},{28,0},{1,5},{5... | collective-permute-start | bytes 3145736 | tf_op jit(solution)/shard_map/ppermute | solution.py:25
  36.8 26.7 %collective-permute-start.1 = (bf16[256,2048]{1,0:T(8,128)(2,1)S(1)}, bf16[256,2048]{1,0:T(8,128)(2,1)}, u32[]{:S(2)}, u32[]{:S(2)}) collective-permute-start(bf16[256,2048]{1,0:T(8,128)(2,1)S(1)} %collective-permute-done), channel_id=1, source_target_pairs={{0,4},{4,8},{8,12},{12,16},{16,20},{20,24},{24,28},{28,0},{1,5},{5... | collective-permute-start | bytes 3145736 | tf_op jit(solution)/shard_map/ppermute | solution.py:25
  48.5 220.6 %copy-start.22 = (f32[128]{0:T(128)}, f32[128]{0:T(128)S(1)}, u32[]{:S(2)}) copy-start(f32[128]{0:T(128)S(1)} %add_rsqrt_fusion.1) | copy-start | bytes 1540
  63.5 29.4 %collective-permute-start.2 = (bf16[256,2048]{1,0:T(8,128)(2,1)}, bf16[256,2048]{1,0:T(8,128)(2,1)S(1)}, u32[]{:S(2)}, u32[]{:S(2)}) collective-permute-start(bf16[256,2048]{1,0:T(8,128)(2,1)} %collective-permute-done.1), channel_id=1, source_target_pairs={{0,4},{4,8},{8,12},{12,16},{16,20},{20,24},{24,28},{28,0},{1,5},{5... | collective-permute-start | bytes 3145736 | tf_op jit(solution)/shard_map/ppermute | solution.py:25
  66.9 208.2 %copy-start.18 = (f32[128,32]{0,1:T(8,128)}, f32[128,32]{0,1:T(8,128)S(1)}, u32[]{:S(2)}) copy-start(f32[128,32]{0,1:T(8,128)S(1)} %get-tuple-element.67) | copy-start | bytes 49156
  66.9 208.2 %copy-start.20 = (f32[128,32]{0,1:T(8,128)}, f32[128,32]{0,1:T(8,128)S(1)}, u32[]{:S(2)}) copy-start(f32[128,32]{0,1:T(8,128)S(1)} %get-tuple-element.68) | copy-start | bytes 49156
  93.0 67.9 %copy-start.12 = (bf16[256,2048]{1,0:T(8,128)(2,1)}, bf16[256,2048]{1,0:T(8,128)(2,1)S(1)}, u32[]{:S(2)}) copy-start(bf16[256,2048]{1,0:T(8,128)(2,1)S(1)} %collective-permute-done.2) | copy-start | bytes 3145732
  93.0 65.4 %collective-permute-start.3 = (bf16[256,2048]{1,0:T(8,128)(2,1)S(1)}, bf16[256,2048]{1,0:T(8,128)(2,1)}, u32[]{:S(2)}, u32[]{:S(2)}) collective-permute-start(bf16[256,2048]{1,0:T(8,128)(2,1)S(1)} %collective-permute-done.2), channel_id=1, source_target_pairs={{0,4},{4,8},{8,12},{12,16},{16,20},{20,24},{24,28},{28,0},{1,5},{5... | collective-permute-start | bytes 3145736 | tf_op jit(solution)/shard_map/ppermute | solution.py:25
  155.0 114.1 %copy-start.13 = (f32[2048]{0:T(1024)}, f32[2048]{0:T(1024)S(1)}, u32[]{:S(2)}) copy-start(f32[2048]{0:T(1024)S(1)} %convert_element_type.206) | copy-start | bytes 24580
  158.4 29.6 %collective-permute-start.4 = (bf16[256,2048]{1,0:T(8,128)(2,1)}, bf16[256,2048]{1,0:T(8,128)(2,1)}, u32[]{:S(2)}, u32[]{:S(2)}) collective-permute-start(bf16[256,2048]{1,0:T(8,128)(2,1)} %collective-permute-done.3), channel_id=1, source_target_pairs={{0,4},{4,8},{8,12},{12,16},{16,20},{20,24},{24,28},{28,0},{1,5},{5... | collective-permute-start | bytes 3145736 | tf_op jit(solution)/shard_map/ppermute | solution.py:25
  184.1 91.2 %copy-start.6 = (bf16[1,512,512]{1,2,0:T(8,128)(2,1)}, bf16[1,512,512]{1,2,0:T(8,128)(2,1)S(1)}, u32[]{:S(2)}) copy-start(bf16[1,512,512]{1,2,0:T(8,128)(2,1)S(1)} %all_gather.47) | copy-start | bytes 1572868
  187.9 158.3 %collective-permute-start.5 = (bf16[256,2048]{1,0:T(8,128)(2,1)}, bf16[256,2048]{1,0:T(8,128)(2,1)}, u32[]{:S(2)}, u32[]{:S(2)}) collective-permute-start(bf16[256,2048]{1,0:T(8,128)(2,1)} %collective-permute-done.4), channel_id=1, source_target_pairs={{0,4},{4,8},{8,12},{12,16},{16,20},{20,24},{24,28},{28,0},{1,5},{5... | collective-permute-start | bytes 3145736 | tf_op jit(solution)/shard_map/ppermute | solution.py:25
  282.8 60.0 %copy-start.4 = (bf16[8,64,4,128]{3,1,2,0:T(8,128)(2,1)}, bf16[8,64,4,128]{3,1,2,0:T(8,128)(2,1)S(1)}, u32[]{:S(2)}) copy-start(bf16[8,64,4,128]{3,1,2,0:T(8,128)(2,1)S(1)} %fusion.24) | copy-start | bytes 1572868
  343.8 361.6 %reduce-scatter.16.cloned.1.call-start = ((), (), s32[]{:S(2)}) async-start(), calls=%async_computation.17 | async-start | bytes 2621440 | tf_op jit(solution)/shard_map/reduce_scatter | solution.py:212
  346.2 24.9 %collective-permute-start.6 = (bf16[256,2048]{1,0:T(8,128)(2,1)}, bf16[256,2048]{1,0:T(8,128)(2,1)S(1)}, u32[]{:S(2)}, u32[]{:S(2)}) collective-permute-start(bf16[256,2048]{1,0:T(8,128)(2,1)} %collective-permute-done.5), channel_id=1, source_target_pairs={{0,4},{4,8},{8,12},{12,16},{16,20},{20,24},{24,28},{28,0},{1,5},{5... | collective-permute-start | bytes 3145736 | tf_op jit(solution)/shard_map/ppermute | solution.py:25
  671.2 64.4 %reduce-scatter.14.cloned.1.call-start = ((), (), s32[]{:S(2)}) async-start(), calls=%async_computation.15 | async-start | bytes 2621440 | tf_op jit(solution)/shard_map/reduce_scatter | solution.py:187
  681.1 108.1 %reduce-scatter.30.cloned.1.call-start = ((), (), s32[]{:S(2)}) async-start(), calls=%async_computation.25 | async-start | bytes 655360
  758.1 46.4 %reduce-scatter.28.cloned.1.call-start = ((), (), s32[]{:S(2)}) async-start(), calls=%async_computation.24 | async-start | bytes 655360
  771.1 440.6 %reduce-scatter.26.cloned.1.call-start = ((), (), s32[]{:S(2)}) async-start(), calls=%async_computation.22 | async-start | bytes 28311552 | tf_op jit(solution)/shard_map/reduce_scatter | solution.py:196
  789.2 535.6 %reduce-scatter.22.cloned.1.call-start = ((), (), s32[]{:S(2)}) async-start(), calls=%async_computation.20 | async-start | bytes 4325376 | tf_op jit(solution)/shard_map/reduce_scatter | solution.py:303
  793.4 672.9 %reduce-scatter.20.cloned.1.call-start = ((), (), s32[]{:S(2)}) async-start(), calls=%async_computation.19 | async-start | bytes 4325376 | tf_op jit(solution)/shard_map/reduce_scatter | solution.py:302
  808.7 874.3 %reduce-scatter.24.cloned.1.call-start = ((), (), s32[]{:S(2)}) async-start(), calls=%async_computation.21 | async-start | bytes 17301504 | tf_op jit(solution)/shard_map/reduce_scatter | solution.py:304
  817.7 1052.6 %reduce-scatter.18.cloned.1.call-start = ((), (), s32[]{:S(2)}) async-start(), calls=%async_computation.18 | async-start | bytes 17301504 | tf_op jit(solution)/shard_map/reduce_scatter | solution.py:301
  (27 other events, 260.1 us)
Sparse Core Ops, SparseCore 0:
  10.9 81.6 all-gather.10
  95.4 68.9 all-gather.12
  167.3 89.4 all-gather.14
  259.5 78.5 all-gather.16
  339.4 21.1 all-gather.22
  362.5 122.4 all-gather.20
  487.1 122.6 all-gather.18
  611.9 24.4 all-gather.24
  671.3 30.6 reduce-scatter.15
  704.3 31.1 reduce-scatter.13
  758.2 21.6 reduce-scatter.29
  782.8 21.6 reduce-scatter.27
  808.4 403.1 reduce-scatter.25
  1214.3 110.4 reduce-scatter.21
  1327.5 138.6 reduce-scatter.19
  1468.9 213.9 reduce-scatter.23
  1685.7 184.6 reduce-scatter.17
